TPU v7x, 256 devices: a whole 4x4x8 slice. The times are simulated.
256 devices in a mesh: seq: 64 (over z, x, core), tp: 4 (over y).
Axes of the slice: x: 4, y: 4, z: 8, core: 2. Of those that a mesh axis runs over, the one named last changes fastest.
Arguments:
- queries: bfloat16 [16384, 4096], P('seq', 'tp'), may hold values from -6 to 6
- vocab_rows: bfloat16 [131072, 1024], P('seq', 'tp'), may hold values from -36 to 36
- neighbour_ids: int32 [256, 2, 128], P('seq'), may hold values from 0 to 131071, as said below
- w_in: bfloat16 [1024, 4096], P(None, 'tp'), may hold values from -0.1875 to 0.1875
- w_out: bfloat16 [4096, 1024], P('tp'), may hold values from -0.09375 to 0.09375
- w_key: bfloat16 [1024, 4096], P(None, 'tp'), may hold values from -0.1875 to 0.1875
- w_value: bfloat16 [1024, 4096], P(None, 'tp'), may hold values from -0.1875 to 0.1875
Outputs:
- cross_out: bfloat16 [16384, 4096], P('seq', 'tp')
Inputs may be any that keep to these rules, and one draw needn't show every extreme that they name: `neighbour_ids`: the owner of id i is i // 2048. Among the neighbour ids of the groups of one index of seq, at most 32 have one owner; some owner has exactly 32 among those of every index.
All inputs are finite; a program needn't handle non-finite values.
Results may differ from a plain program's by a relative error of at most 0.0095.
Values may be sent and summed in bfloat16 or wider, within the bound.
A program may use at most 64 MiB of HBM per device.

v0:
```python
import jax
import jax.numpy as jnp
from jax import lax
from jax.sharding import PartitionSpec as P

HEAD_WIDTH = 128
GROUP = 64


def shifted(x, axis, by):
    length = lax.axis_size(axis)
    pairs = [(i, i + by) for i in range(length) if 0 <= i + by < length]
    return lax.ppermute(x, axis, pairs)


def attend_blocks(q_blocks, paired):
    blocks, count, width = q_blocks.shape
    heads = width // HEAD_WIDTH
    kcount = paired.shape[2]
    decoder_query = q_blocks.reshape(blocks, count, heads, HEAD_WIDTH)
    neighbour_key_heads = paired[0].reshape(blocks, kcount, heads, HEAD_WIDTH)
    neighbour_value_heads = paired[1].reshape(blocks, kcount, heads, HEAD_WIDTH)
    attention_logits = jnp.einsum(
        "bmhd,bkhd->bhmk", decoder_query, neighbour_key_heads, preferred_element_type=jnp.float32
    ) * HEAD_WIDTH ** (-0.5)
    expo = jnp.exp(attention_logits)
    attention_probs = (expo / jnp.sum(expo, axis=-1, keepdims=True)).astype(jnp.bfloat16)
    attended_values = jnp.einsum(
        "bhmk,bkhd->bmhd",
        attention_probs,
        neighbour_value_heads,
        preferred_element_type=jnp.float32,
    )
    return attended_values.reshape(blocks, count, width).astype(jnp.bfloat16)


def per_device(queries, vocab_rows, neighbour_ids, w_in, w_out, w_key, w_value):
    seq_size = lax.axis_size("seq")
    flat_ids = neighbour_ids.reshape(-1)
    rows = flat_ids.shape[0]
    voc_local = vocab_rows.shape[0]
    capacity = max(2, 2 * rows // seq_size)
    owner = flat_ids // voc_local
    local_row = flat_ids % voc_local
    owner_table = (owner[:, None] == jnp.arange(seq_size, dtype=jnp.int32)[None, :]).astype(
        jnp.int32
    )
    rank = jnp.sum((jnp.cumsum(owner_table, axis=0) - 1) * owner_table, axis=1)
    slot = owner * capacity + rank
    wanted = (
        jnp.zeros((seq_size * capacity,), jnp.int32)
        .at[slot]
        .set(local_row)
        .reshape(seq_size, capacity)
    )
    found = jnp.take(
        vocab_rows, lax.all_to_all(wanted, "seq", split_axis=0, concat_axis=0, tiled=True), axis=0
    )
    answered = lax.all_to_all(found, "seq", split_axis=0, concat_axis=0, tiled=True)
    own_rows = answered[owner, rank]
    gathered = lax.all_gather(own_rows, "tp", axis=1, tiled=True)
    values_f = gathered.astype(jnp.float32)
    normed = (
        values_f * lax.rsqrt(jnp.mean(values_f * values_f, axis=-1, keepdims=True) + 1e-06)
    ).astype(jnp.bfloat16)
    inner = jax.nn.gelu(
        jnp.dot(normed, w_in, preferred_element_type=jnp.float32), approximate=True
    ).astype(jnp.bfloat16)
    total = lax.psum(jnp.dot(inner, w_out, preferred_element_type=jnp.float32), "tp")
    encoded = (values_f + total).astype(jnp.bfloat16)
    keys = jnp.dot(encoded, w_key, preferred_element_type=jnp.float32).astype(jnp.bfloat16)
    values = jnp.dot(encoded, w_value, preferred_element_type=jnp.float32).astype(jnp.bfloat16)
    groups = neighbour_ids.shape[0]
    per_group = neighbour_ids.shape[1] * neighbour_ids.shape[2]
    width = queries.shape[1]
    paired = jnp.stack([keys, values]).reshape(2, groups, per_group, width)
    tok = queries.shape[0]
    edge = GROUP - 1
    behind = shifted(paired[:, groups - 1], "seq", 1)
    local_q = jnp.concatenate([queries[edge:], jnp.zeros((edge, width), queries.dtype)], axis=0)
    windows = attend_blocks(local_q.reshape(groups, GROUP, width), paired)
    head = attend_blocks(queries[:edge][None], behind[:, None])[0]
    flat = windows.reshape(tok, width)[: tok - edge]
    at_start = lax.axis_index("seq") == 0
    head = jnp.where(at_start, jnp.zeros_like(head), head)
    return jnp.concatenate([head, flat], axis=0)


def solution(mesh):
    return jax.shard_map(
        per_device,
        mesh=mesh,
        in_specs=(
            P("seq", "tp"),
            P("seq", "tp"),
            P("seq", None, None),
            P(None, "tp"),
            P("tp", None),
            P(None, "tp"),
            P(None, "tp"),
        ),
        out_specs=P("seq", "tp"),
        check_vma=False,
    )
```

profile of v0, /device:TPU:32, one launch (start us, length us, event | category | flops | bytes accessed | tf_op | source)
XLA Modules:
  0.0 318.1 jit_solution(9395363509279118704)
XLA Ops:
  6.5 0.0 copy-start
  6.5 0.0 copy-start.5
  6.5 0.0 copy-start.1
  6.5 0.0 all-gather.2.cloned.1.call-start
  6.5 0.8 add_select_fusion.1
  7.4 0.7 add_select_fusion
  8.1 0.7 fusion.47
  8.9 31.1 %reduce-window.6 = s32[64,8,128]{2,1,0:T(8,128)S(1)} reduce-window(s32[64,8,128]{2,1,0:T(8,128)} %fusion.47, s32[]{:T(128)} %constant.37.clone.1), window={size=1x1x128 pad=0_0x0_0x127_0}, to_apply=%region_0.1 | reduce-window | flops 8323072 | bytes 524292 | tf_op jit(solution)/shard_map/reduce-window
  40.0 0.8 slice.42
  40.8 1.1 copy.22
  41.9 0.1 copy.23
  42.0 0.1 add_add_fusion
  42.1 0.1 fusion.44
  42.2 0.0 copy-done.5
  42.3 4.3 %scatter_custom_fusion = s32[2048]{0:T(1024)S(1)} fusion(s32[1024]{0:T(1024)S(1)} %bitcast.100, s32[1024]{0:T(1024)S(1)} %get-tuple-element.9, s32[]{:T(128)} %constant.37.clone.1), kind=kCustom, calls=%fused_computation.91 | custom fusion | bytes 8196 | tf_op jit(solution)/shard_map/scatter | solution.py:53
  46.6 0.1 all_to_all.13
  46.7 20.0 %all_to_all.20 = s32[64,1,32]{2,1,0:T(1,128)S(1)} all-to-all(s32[64,1,32]{2,1,0:T(1,128)S(1)} %bitcast.93), channel_id=1, replica_groups=mesh['seq'=64,'tp'=4] {'seq'}, dimensions={0} | all-to-all | bytes 16384 | tf_op jit(solution)/shard_map/all_to_all | solution.py:57
  66.8 0.1 reshape.275
  66.8 0.0 copy-done.1
  66.8 9.0 %gather_fusion = bf16[2048,256]{1,0:T(8,128)(2,1)} fusion(bf16[2048,256]{1,0:T(8,128)(2,1)S(1)} %copy-done.1, s32[2048]{0:T(1024)S(1)} %broadcast_clamp_fusion), kind=kCustom, calls=%fused_computation | custom fusion | bytes 2105344 | tf_op jit(solution)/shard_map/jit(_take)/gather | solution.py:56
  75.8 1.5 broadcast_select_fusion
  77.3 32.7 %all_to_all.21 = bf16[64,32,256]{2,1,0:T(8,128)(2,1)S(1)} all-to-all(bf16[64,32,256]{2,1,0:T(8,128)(2,1)S(1)} %broadcast_select_fusion), channel_id=1, replica_groups=mesh['seq'=64,'tp'=4] {'seq'}, dimensions={0} | all-to-all | bytes 2097152 | tf_op jit(solution)/shard_map/all_to_all | solution.py:59
  110.0 10.7 %gather_fusion.1 = bf16[1024,256]{1,0:T(8,128)(2,1)} fusion(bf16[64,32,256]{2,1,0:T(8,128)(2,1)S(1)} %all_to_all.21, s32[1024]{0:T(1024)S(1)} %bitcast.72), kind=kCustom, calls=%fused_computation.1 | custom fusion | bytes 1056768 | tf_op jit(solution)/shard_map/gather | solution.py:60
  120.7 0.0 all-gather.2.cloned.1.call-update
  120.7 0.2 all-reduce.3.cloned.1.call-start
  121.0 34.0 %all-gather.2.cloned.1.call-done = bf16[1024,1024]{1,0:T(8,128)(2,1)} async-done(((bf16[1024,256]{1,0:T(8,128)(2,1)}), bf16[1024,1024]{1,0:T(8,128)(2,1)}) %all-gather.2.cloned.1.call-update) | async-done | bytes 2097168 | tf_op jit(solution)/shard_map/all_gather | solution.py:61
  155.0 2.1 fusion
  157.1 0.0 copy-done
  157.1 8.8 %fusion.11 = f32[1024,1024]{1,0:T(8,128)} fusion(bf16[1024,1024]{1,0:T(8,128)(2,1)S(1)} %copy-done, bf16[1024,1024]{1,0:T(8,128)(2,1)} %param.10, bf16[1024,1024]{1,0:T(8,128)(2,1)} %all-gather.2.cloned.1.call-done, f32[1024]{0:T(1024)S(1)} %add_rsqrt_fusion), kind=kOutput, calls=%fused_computation.18 | convolution fusion | flops 4307550208 | bytes 10489856 | tf_op jit(solution)/shard_map/dot_general | solution.py:69
  165.9 0.0 all-reduce.3.cloned.1.call-update
  165.9 99.0 %all-reduce.3.cloned.1.call-done = f32[1024,1024]{1,0:T(8,128)} async-done(((f32[1024,1024]{1,0:T(8,128)}), f32[1024,1024]{1,0:T(8,128)}) %all-reduce.3.cloned.1.call-update) | async-done | bytes 4194320 | tf_op jit(solution)/shard_map/psum | solution.py:69
  265.0 7.1 %convolution_convert_fusion = bf16[1024,1024]{1,0:T(8,128)(2,1)} fusion(bf16[1024,1024]{1,0:T(8,128)(2,1)} %param.13, f32[1024,1024]{1,0:T(8,128)} %all-reduce.3.cloned.1.call-done, bf16[1024,1024]{1,0:T(8,128)(2,1)} %all-gather.2.cloned.1.call-done), kind=kOutput, calls=%fused_computation.31 | convolution fusion | flops 2151677952 | bytes 10485760 | tf_op jit(solution)/shard_map/dot_general | solution.py:72
  272.1 4.0 %copy.26 = bf16[1,4,256,1024]{2,3,0,1:T(8,128)(2,1)} copy(bf16[1,4,256,1024]{3,2,1,0:T(8,128)(2,1)} %bitcast.73) | data formatting | bytes 4194304 | tf_op jit(solution)/shard_map/stack | solution.py:76
  276.0 7.1 %convolution_convert_fusion.1 = bf16[1024,1024]{1,0:T(8,128)(2,1)} fusion(bf16[1024,1024]{1,0:T(8,128)(2,1)} %param.12, f32[1024,1024]{1,0:T(8,128)} %all-reduce.3.cloned.1.call-done, bf16[1024,1024]{1,0:T(8,128)(2,1)} %all-gather.2.cloned.1.call-done), kind=kOutput, calls=%fused_computation.32 | convolution fusion | flops 2151677952 | bytes 10485760 | tf_op jit(solution)/shard_map/dot_general | solution.py:71
  283.1 3.9 %copy.25 = bf16[1,4,256,1024]{2,3,0,1:T(8,128)(2,1)} copy(bf16[1,4,256,1024]{3,2,1,0:T(8,128)(2,1)} %bitcast.75) | data formatting | bytes 4194304 | tf_op jit(solution)/shard_map/stack | solution.py:76
  287.1 0.0 copy-start.4
  287.1 1.4 fusion.39
  288.4 2.1 collective-permute-start
  290.6 0.0 copy-done.4
  290.6 0.7 slice.35
  291.3 0.1 slice.36
  291.4 0.0 copy-start.2
  291.4 1.1 copy.38
  292.5 0.1 pad_bitcast_fusion
  292.5 0.1 copy.40
  292.6 0.4 copy-done.2
  293.0 0.0 copy-start.3
  293.0 0.6 copy.42
  293.7 1.0 copy-done.3
  294.6 0.6 copy.41
  295.3 0.9 fusion.24
  296.2 0.8 fusion.28
  297.0 0.3 copy.34
  297.3 0.1 copy.63
  297.5 9.3 %collective-permute-done = bf16[2,256,1024]{1,2,0:T(8,128)(2,1)} collective-permute-done((bf16[2,256,1024]{1,2,0:T(8,128)(2,1)S(1)}, bf16[2,256,1024]{1,2,0:T(8,128)(2,1)}, u32[]{:S(2)}, u32[]{:S(2)}) %collective-permute-start) | collective-permute-done | bytes 1048608 | tf_op jit(solution)/shard_map/ppermute | solution.py:13
  306.8 1.3 fusion.68
  308.0 0.2 fusion.32
  308.3 1.0 fusion.34
  309.3 1.0 copy.64
  310.3 0.9 pad_maximum_fusion.1
  (12 shorter events, 0.2 us)
Async XLA Ops:
  6.5 150.6 %copy-start = (bf16[1024,1024]{1,0:T(8,128)(2,1)S(1)}, bf16[1024,1024]{1,0:T(8,128)(2,1)}, u32[]{:S(2)}) copy-start(bf16[1024,1024]{1,0:T(8,128)(2,1)} %param.11) | copy-start | bytes 6291460
  6.5 35.7 %copy-start.5 = (s32[4,2,128]{2,1,0:T(2,128)S(1)}, s32[4,2,128]{2,1,0:T(2,128)}, u32[]{:S(2)}) copy-start(s32[4,2,128]{2,1,0:T(2,128)} %param.9) | copy-start | bytes 12292
  6.5 60.3 %copy-start.1 = (bf16[2048,256]{1,0:T(8,128)(2,1)S(1)}, bf16[2048,256]{1,0:T(8,128)(2,1)}, u32[]{:S(2)}) copy-start(bf16[2048,256]{1,0:T(8,128)(2,1)} %param.8) | copy-start | bytes 3145732
  6.5 148.5 %all-gather.2.cloned.1.call-start = ((), (), s32[]{:S(2)}) async-start(), calls=%async_computation.2 | async-start | bytes 2621440 | tf_op jit(solution)/shard_map/all_gather | solution.py:61
  120.7 144.2 %all-reduce.3.cloned.1.call-start = ((), (), s32[]{:S(2)}) async-start(), calls=%async_computation.3 | async-start | bytes 8388608 | tf_op jit(solution)/shard_map/psum | solution.py:69
  287.1 3.5 %copy-start.4 = (bf16[256,1024]{1,0:T(8,128)(2,1)S(1)}, bf16[256,1024]{1,0:T(8,128)(2,1)}, u32[]{:S(2)}) copy-start(bf16[256,1024]{1,0:T(8,128)(2,1)} %param.7) | copy-start | bytes 1572868
  288.4 18.3 %collective-permute-start = (bf16[2,256,1024]{1,2,0:T(8,128)(2,1)S(1)}, bf16[2,256,1024]{1,2,0:T(8,128)(2,1)}, u32[]{:S(2)}, u32[]{:S(2)}) collective-permute-start(bf16[2,256,1024]{1,2,0:T(8,128)(2,1)S(1)} %fusion.39), channel_id=1, source_target_pairs={{0,4},{4,8},{8,12},{12,16},{16,20},{20,24},{24,28},{28,32},{32,36}... | collective-permute-start | bytes 3145736 | tf_op jit(solution)/shard_map/ppermute | solution.py:13
  291.4 1.7 copy-start.2
  293.0 1.6 copy-start.3
Sparse Core Ops, SparseCore 0:
  120.9 34.1 all-gather.1
  166.0 98.8 all-reduce.2
where the time goes:
time: 320 us; the launch traced here: 318 us
  waiting for transfers between devices  142 us (44%)
  blocking collectives  52.7 us (16%)
  local copies, waits for them, and re-layouts  41.4 us (13%)
  other arithmetic  39.5 us (12%)
  matrix products  26 us (8%)
  between operations  13.7 us (4%)
    psum x1, waiting for transfers between devices, per_device(): lax.psum(jnp.dot(inner, w_out, preferred_element_type=jnp.float32), 'tp')  99 us
    all_gather x1, waiting for transfers between devices, per_device(): gathered = lax.all_gather(own_rows, 'tp', axis=1, tiled=True)  34 us
    all_to_all x1, blocking collectives, per_device(): lax.all_to_all(found, 'seq', split_axis=0, concat_axis=0, tiled=True)  32.7 us
    another operation x2, other arithmetic  31.1 us
    all_to_all x1, blocking collectives, per_device(): lax.all_to_all(wanted, 'seq', split_axis=0, concat_axis=0, tiled=True)  20 us
    gather x1, local copies, waits for them, and re-layouts, per_device(): own_rows = answered[owner, rank]  10.7 us
    ppermute x1, waiting for transfers between devices, shifted(): return lax.ppermute(x, axis, pairs)  9.3 us
    gather x1, local copies, waits for them, and re-layouts, per_device(): jnp.take(vocab_rows, lax.all_to_all(wanted, 'seq', split_axis=0, concat_a...  9 us
  transfers between devices with their start and end apart: 3, of which 3 were waited for; matrix products, arithmetic and copies ran while one was open for 2% of the time, Pallas kernels for 0%

commit v1 on v0

v1 whole, which is shorter than its diff:
```python
import functools

import jax
import jax.numpy as jnp
from jax import lax
from jax.experimental import pallas as pl
from jax.experimental.pallas import tpu as pltpu
from jax.sharding import PartitionSpec as P

HEAD_WIDTH = 128
GROUP = 64
F32 = jnp.float32
BF16 = jnp.bfloat16
MESH = pl.DeviceIdType.MESH
NT = (((1,), (1,)), ((), ()))


def mm(a, b):
    return jnp.dot(a, b, preferred_element_type=F32)


def rows_kernel(n, plane, cap, ids_ref, vocab_ref, out_ref, want, req, sendb, recvb, acc, slots,
                isend, irecv, rsend, rrecv):
    me = lax.axis_index("seq")
    planes = n // plane
    mine = me // plane
    rows = ids_ref.shape[1]
    voc, feats = vocab_ref.shape
    block = plane * cap
    shift = voc.bit_length() - 1

    barrier = pltpu.get_barrier_semaphore()

    def greet(k, c):
        pl.semaphore_signal(barrier, inc=1, device_id={"seq": lax.rem(me + k, n)}, device_id_type=MESH)
        return c

    lax.fori_loop(1, n, greet, 0)

    ids = ids_ref[...]
    owner = ids >> shift
    local = ids & (voc - 1)
    hot = jnp.where(lax.broadcasted_iota(jnp.int32, (n, rows), 0) == owner, 1.0, 0.0).astype(F32)
    hot16 = hot.astype(BF16)
    before = jnp.where(
        lax.broadcasted_iota(jnp.int32, (rows, rows), 0) < lax.broadcasted_iota(jnp.int32, (rows, rows), 1), 1.0, 0.0
    ).astype(BF16)
    count = mm(hot16, before)
    rank = jnp.sum(hot * count, axis=0, keepdims=True).astype(jnp.int32)
    ranked = lax.broadcasted_iota(jnp.int32, (128, rows), 0) == rank
    low = jnp.where(ranked, (local & 255).astype(F32), 0.0).astype(BF16)
    high = jnp.where(ranked, (local >> 8).astype(F32), 0.0).astype(BF16)
    table = lax.dot_general(hot16, low, NT, preferred_element_type=F32) + 256.0 * lax.dot_general(
        hot16, high, NT, preferred_element_type=F32
    )
    table = table.astype(jnp.int32)
    for o in range(n):
        want[o] = table[o : o + 1]

    pl.semaphore_wait(barrier, n - 1)

    def ids_copy(peer):
        return pltpu.make_async_remote_copy(
            src_ref=want.at[peer], dst_ref=req.at[me], send_sem=isend.at[peer], recv_sem=irecv.at[me],
            device_id={"seq": peer}, device_id_type=MESH,
        )

    def ids_arrival(src):
        return pltpu.make_async_remote_copy(
            src_ref=want.at[src], dst_ref=req.at[src], send_sem=isend.at[src], recv_sem=irecv.at[src],
            device_id={"seq": src}, device_id_type=MESH,
        )

    def rows_copy(peer):
        return pltpu.make_async_remote_copy(
            src_ref=sendb.at[peer], dst_ref=recvb.at[me], send_sem=rsend.at[peer], recv_sem=rrecv.at[me],
            device_id={"seq": peer}, device_id_type=MESH,
        )

    def rows_arrival(src):
        return pltpu.make_async_remote_copy(
            src_ref=sendb.at[src], dst_ref=recvb.at[src], send_sem=rsend.at[src], recv_sem=rrecv.at[src],
            device_id={"seq": src}, device_id_type=MESH,
        )

    def step_of(i):
        half = (i + 1) // 2
        return lax.rem(planes // 2 + jnp.where(lax.rem(i, 2) == 1, -half, half) + planes, planes)

    def send_ids(i, c):
        to = lax.rem(mine + step_of(i), planes)
        for j in range(plane):
            peer = to * plane + j

            @pl.when(peer != me)
            def _():
                ids_copy(peer).start()

        return c

    lax.fori_loop(0, planes, send_ids, 0)
    req[me] = want[me]

    slot = (owner * cap + rank).astype(F32)
    slots[...] = jnp.transpose(jnp.broadcast_to(slot, (128, rows)))

    def answer(i, c):
        to = lax.rem(mine + step_of(i), planes)
        for j in range(plane):
            peer = to * plane + j

            @pl.when(peer != me)
            def _():
                ids_arrival(peer).wait_recv()

        asked = jnp.concatenate([req[to * plane + j] for j in range(plane)], axis=0).astype(F32)
        asked = jnp.transpose(jnp.concatenate([asked, jnp.zeros((128 - plane, 128), F32)], axis=0))
        cols = [jnp.broadcast_to(asked[:cap, j : j + 1], (cap, 128)) for j in range(plane)]
        col = jnp.concatenate(cols, axis=0)
        total = jnp.zeros((block, feats), F32)
        deep = min(256, voc)
        for v in range(0, voc, deep):
            picks = [
                jnp.where(
                    col == (lax.broadcasted_iota(jnp.int32, (block, 128), 1) + (v + w)).astype(F32), 1.0, 0.0
                ).astype(BF16)
                for w in range(0, deep, 128)
            ]
            total += mm(jnp.concatenate(picks, axis=1), vocab_ref[v : v + deep, :])
        found = total.astype(BF16)
        for j in range(plane):
            sendb[to * plane + j] = found[j * cap : (j + 1) * cap]
        for j in range(plane):
            peer = to * plane + j

            @pl.when(peer != me)
            def _():
                rows_copy(peer).start()

        return c

    lax.fori_loop(0, planes, answer, 0)
    recvb[me] = sendb[me]

    acc[...] = jnp.zeros_like(acc)

    def gather(i, c):
        source = lax.rem(mine - step_of(i) + planes, planes)
        for j in range(plane):
            src = source * plane + j

            @pl.when(src != me)
            def _():
                rows_arrival(src).wait_recv()

        first = (source * block).astype(F32)
        at = slots[...] - first
        picks = [
            jnp.where(at == (lax.broadcasted_iota(jnp.int32, (rows, 128), 1) + w).astype(F32), 1.0, 0.0).astype(BF16)
            for w in range(0, block, 128)
        ]
        got = jnp.concatenate([recvb[source * plane + j] for j in range(plane)], axis=0)
        acc[...] += mm(jnp.concatenate(picks, axis=1), got)
        return c

    lax.fori_loop(0, planes, gather, 0)
    out_ref[...] = acc[...].astype(BF16)

    def drain(k, c):
        peer = lax.rem(me + k, n)
        ids_copy(peer).wait_send()
        rows_copy(peer).wait_send()
        return c

    lax.fori_loop(1, n, drain, 0)


def fetch_rows(ids, vocab_rows, n, plane, cap):
    rows = ids.shape[1]
    feats = vocab_rows.shape[1]
    return pl.pallas_call(
        functools.partial(rows_kernel, n, plane, cap),
        out_shape=jax.ShapeDtypeStruct((rows, feats), BF16),
        in_specs=[pl.BlockSpec(memory_space=pltpu.VMEM)] * 2,
        out_specs=pl.BlockSpec(memory_space=pltpu.VMEM),
        scratch_shapes=[
            pltpu.VMEM((n, 1, 128), jnp.int32),
            pltpu.VMEM((n, 1, 128), jnp.int32),
            pltpu.VMEM((n, cap, feats), BF16),
            pltpu.VMEM((n, cap, feats), BF16),
            pltpu.VMEM((rows, feats), F32),
            pltpu.VMEM((rows, 128), F32),
            pltpu.SemaphoreType.DMA((n,)),
            pltpu.SemaphoreType.DMA((n,)),
            pltpu.SemaphoreType.DMA((n,)),
            pltpu.SemaphoreType.DMA((n,)),
        ],
        compiler_params=pltpu.CompilerParams(collective_id=0, has_side_effects=True),
    )(ids, vocab_rows)


def layer_kernel(n, groups, x_ref, q_ref, win_hbm, wout_hbm, wk_hbm, wv_hbm, out_ref,
                 win, wout, wk, wv, xb, eb, hop_r, hop_l, via_r, via_l, to_r, to_l, from_l, from_r, part, mine_p,
                 qnext, wins, head, wsem, xs, xr, es, er, rs, rr, qs, qr, hs, hr):
    tp = 4
    t = lax.axis_index("tp")
    s = lax.axis_index("seq")
    right, left, across = lax.rem(t + 1, tp), lax.rem(t + tp - 1, tp), lax.rem(t + 2, tp)
    ahead, back = lax.rem(s + 1, n), lax.rem(s + n - 1, n)
    keys = x_ref.shape[1]
    fs = x_ref.shape[2]
    width = q_ref.shape[1]
    half = keys // 2
    hidden = win.shape[1]
    heads = width // HEAD_WIDTH

    loads = [
        pltpu.make_async_copy(a, b, wsem.at[i])
        for i, (a, b) in enumerate([(win_hbm, win), (wout_hbm, wout), (wk_hbm, wk), (wv_hbm, wv)])
    ]
    for load in loads:
        load.start()

    barrier = pltpu.get_barrier_semaphore()
    for where in ({"tp": right}, {"tp": left}, {"seq": ahead}, {"seq": back}):
        pl.semaphore_signal(barrier, inc=1, device_id=where, device_id_type=MESH)
    pl.semaphore_wait(barrier, 4)

    def remote(src, dst, ssem, rsem, where):
        return pltpu.make_async_remote_copy(
            src_ref=src, dst_ref=dst, send_sem=ssem, recv_sem=rsem, device_id=where, device_id_type=MESH
        )

    RIGHT, LEFT = {"tp": right}, {"tp": left}

    def ring(buf, ssem, rsem, g):
        own = buf.at[g, 0]
        return dict(
            own_r=remote(own, buf.at[g, 1], ssem.at[g, 0], rsem.at[g, 0], RIGHT),
            own_l=remote(own, buf.at[g, 2], ssem.at[g, 1], rsem.at[g, 1], LEFT),
            fwd_r=remote(buf.at[g, 1, pl.ds(0, half)], buf.at[g, 3, pl.ds(0, half)], ssem.at[g, 2], rsem.at[g, 2], RIGHT),
            fwd_l=remote(buf.at[g, 2, pl.ds(half, half)], buf.at[g, 3, pl.ds(half, half)], ssem.at[g, 3], rsem.at[g, 3], LEFT),
        )

    gather_x = [ring(xb, xs, xr, g) for g in range(groups)]
    gather_e = [ring(eb, es, er, g) for g in range(groups)]
    reduce_p = [
        dict(
            hop_r=remote(hop_r.at[g], via_r.at[g], rs.at[g, 0], rr.at[g, 0], RIGHT),
            hop_l=remote(hop_l.at[g], via_l.at[g], rs.at[g, 1], rr.at[g, 1], LEFT),
            raw_r=remote(to_r.at[g, pl.ds(half, half)], from_l.at[g, pl.ds(half, half)], rs.at[g, 2], rr.at[g, 2], RIGHT),
            raw_l=remote(to_l.at[g, pl.ds(0, half)], from_r.at[g, pl.ds(0, half)], rs.at[g, 3], rr.at[g, 3], LEFT),
            sum_r=remote(to_r.at[g, pl.ds(0, half)], from_l.at[g, pl.ds(0, half)], rs.at[g, 4], rr.at[g, 4], RIGHT),
            sum_l=remote(to_l.at[g, pl.ds(half, half)], from_r.at[g, pl.ds(half, half)], rs.at[g, 5], rr.at[g, 5], LEFT),
        )
        for g in range(groups)
    ]
    q_back = remote(q_ref.at[pl.ds(0, GROUP)], qnext, qs.at[0], qr.at[0], {"seq": back})
    head_on = remote(wins.at[groups], head, hs.at[0], hr.at[0], {"seq": ahead})

    slices = [t, left, right, across]

    def feature(i):
        return pl.ds(pl.multiple_of(slices[i] * fs, fs), fs)

    def start_own(table, g):
        table[g]["own_r"].start()
        table[g]["own_l"].start()

    def forward(table, g):
        table[g]["own_r"].wait_recv()
        table[g]["fwd_r"].start()
        table[g]["own_l"].wait_recv()
        table[g]["fwd_l"].start()

    def complete(table, g):
        table[g]["fwd_r"].wait_recv()
        table[g]["fwd_l"].wait_recv()

    def feed(g):
        complete(gather_x, g)
        square = jnp.zeros((keys, 1), F32)
        for i in range(4):
            v = xb[g, i].astype(F32)
            square += jnp.sum(v * v, axis=-1, keepdims=True)
        scale = lax.rsqrt(square * (1.0 / (4 * fs)) + 1e-06)
        hid = jnp.zeros((keys, hidden), F32)
        for i in range(4):
            normed = (xb[g, i].astype(F32) * scale).astype(BF16)
            hid += mm(normed, win[feature(i), :])
        inner = jax.nn.gelu(hid, approximate=True).astype(BF16)
        pa = mm(inner, wout[:, feature(3)])
        hop_r[g] = pa[:half].astype(BF16)
        hop_l[g] = pa[half:].astype(BF16)
        reduce_p[g]["hop_r"].start()
        reduce_p[g]["hop_l"].start()
        pr = mm(inner, wout[:, feature(2)])
        to_r[g, pl.ds(half, half)] = pr[half:].astype(BF16)
        part[g, 0] = pr[:half]
        reduce_p[g]["raw_r"].start()
        pleft = mm(inner, wout[:, feature(1)])
        to_l[g, pl.ds(0, half)] = pleft[:half].astype(BF16)
        part[g, 1] = pleft[half:]
        reduce_p[g]["raw_l"].start()
        mine_p[g] = xb[g, 0].astype(F32) + mm(inner, wout[:, feature(0)])

    def merge(g):
        p = reduce_p[g]
        p["hop_r"].wait_recv()
        to_r[g, pl.ds(0, half)] = (part[g, 0] + via_r[g].astype(F32)).astype(BF16)
        p["sum_r"].start()
        p["hop_l"].wait_recv()
        to_l[g, pl.ds(half, half)] = (part[g, 1] + via_l[g].astype(F32)).astype(BF16)
        p["sum_l"].start()

    def encode(g):
        p = reduce_p[g]
        for name in ("raw_r", "raw_l", "sum_r", "sum_l"):
            p[name].wait_recv()
        eb[g, 0] = (mine_p[g] + from_l[g].astype(F32) + from_r[g].astype(F32)).astype(BF16)
        start_own(gather_e, g)

    scale = HEAD_WIDTH ** (-0.5)

    def shifted(rows_a, count):
        pick = lax.broadcasted_iota(jnp.int32, (GROUP, 2 * GROUP), 1) == (
            lax.broadcasted_iota(jnp.int32, (GROUP, 2 * GROUP), 0) + count
        )
        return mm(jnp.where(pick, 1.0, 0.0).astype(BF16), rows_a).astype(BF16)

    def attend(g):
        complete(gather_e, g)
        kk = jnp.zeros((keys, width), F32)
        for i in range(4):
            kk += mm(eb[g, i], wk[feature(i), :])
        kk = kk.astype(BF16)
        vv = jnp.zeros((keys, width), F32)
        for i in range(4):
            vv += mm(eb[g, i], wv[feature(i), :])
        vv = vv.astype(BF16)
        if g == groups - 1:
            q_back.wait_recv()
            both = jnp.concatenate([q_ref[g * GROUP : (g + 1) * GROUP, :], qnext[...]], axis=0)
        else:
            both = q_ref[g * GROUP : (g + 2) * GROUP, :]
        qg = shifted(both, GROUP - 1)
        for h in range(heads):
            at = slice(h * HEAD_WIDTH, (h + 1) * HEAD_WIDTH)
            logits = lax.dot_general(qg[:, at], kk[:, at], NT, preferred_element_type=F32) * scale
            expo = jnp.exp(logits)
            probs = (expo * (1.0 / jnp.sum(expo, axis=-1, keepdims=True))).astype(BF16)
            wins[g + 1, :, at] = mm(probs, vv[:, at]).astype(BF16)

    order = [groups - 1] + list(range(groups - 1))
    q_back.start()

    A0 = lambda k: start_own(gather_x, order[k])
    A1 = lambda k: forward(gather_x, order[k])
    F = lambda k: feed(order[k])
    M = lambda k: merge(order[k])
    E = lambda k: encode(order[k])
    G = lambda k: forward(gather_e, order[k])
    T = lambda k: attend(order[k])

    for g in range(groups):
        xb[g, 0] = x_ref[g]
    A0(0)
    A0(1)
    loads[0].wait()
    A1(0)
    A0(2)
    A1(1)
    loads[1].wait()
    F(0)
    A0(3)
    A1(2)
    M(0)
    F(1)
    A1(3)
    E(0)
    M(1)
    F(2)
    G(0)
    E(1)
    M(2)
    F(3)
    loads[2].wait()
    loads[3].wait()
    G(1)
    T(0)
    head_on.start()
    E(2)
    M(3)
    T(1)
    G(2)
    E(3)
    T(2)
    G(3)
    head_on.wait_recv()
    at_start = jnp.where(s == 0, 0.0, 1.0)
    wins[0] = jnp.where(at_start > 0.0, head[...].astype(F32), 0.0).astype(BF16)
    T(3)
    for b in range(groups):
        both = jnp.concatenate([wins[b], wins[b + 1]], axis=0)
        out_ref[b * GROUP : (b + 1) * GROUP, :] = shifted(both, 1)
    for table in (gather_x, gather_e, reduce_p):
        for g in range(groups):
            for copy in table[g].values():
                copy.wait_send()
    q_back.wait_send()
    head_on.wait_send()


def run_layer(x, queries, w_in, w_out, w_key, w_value, n):
    groups, keys, fs = x.shape
    tok, width = queries.shape
    half = keys // 2
    vm = lambda shape, dt=BF16: pltpu.VMEM(shape, dt)
    dma = pltpu.SemaphoreType.DMA
    return pl.pallas_call(
        functools.partial(layer_kernel, n, groups),
        out_shape=jax.ShapeDtypeStruct((tok, width), BF16),
        in_specs=[pl.BlockSpec(memory_space=pltpu.VMEM)] * 2 + [pl.BlockSpec(memory_space=pl.ANY)] * 4,
        out_specs=pl.BlockSpec(memory_space=pltpu.VMEM),
        scratch_shapes=[
            vm(w_in.shape), vm(w_out.shape), vm(w_key.shape), vm(w_value.shape),
            vm((groups, 4, keys, fs)), vm((groups, 4, keys, fs)),
            vm((groups, half, fs)), vm((groups, half, fs)), vm((groups, half, fs)), vm((groups, half, fs)),
            vm((groups, keys, fs)), vm((groups, keys, fs)), vm((groups, keys, fs)), vm((groups, keys, fs)),
            vm((groups, 2, half, fs), F32), vm((groups, keys, fs), F32),
            vm((GROUP, width)), vm((groups + 1, GROUP, width)), vm((GROUP, width)),
            dma((4,)), dma((groups, 4)), dma((groups, 4)), dma((groups, 4)), dma((groups, 4)),
            dma((groups, 6)), dma((groups, 6)), dma((1,)), dma((1,)), dma((1,)), dma((1,)),
        ],
        compiler_params=pltpu.CompilerParams(
            collective_id=1, has_side_effects=True, vmem_limit_bytes=48 * 1024 * 1024
        ),
    )(x, queries, w_in, w_out, w_key, w_value)


def per_device(n, queries, vocab_rows, neighbour_ids, w_in, w_out, w_key, w_value):
    groups = neighbour_ids.shape[0]
    ids = neighbour_ids.reshape(1, -1)
    rows = ids.shape[1]
    cap = 2 * rows // n
    plane = 8 if n % 8 == 0 else 2
    own = fetch_rows(ids, vocab_rows, n, plane, cap)
    x = own.reshape(groups, rows // groups, vocab_rows.shape[1])
    return run_layer(x, queries, w_in, w_out, w_key, w_value, n)


def solution(mesh):
    return jax.shard_map(
        functools.partial(per_device, mesh.shape["seq"]),
        mesh=mesh,
        in_specs=(
            P("seq", "tp"),
            P("seq", "tp"),
            P("seq", None, None),
            P(None, "tp"),
            P("tp", None),
            P(None, "tp"),
            P(None, "tp"),
        ),
        out_specs=P("seq", "tp"),
        check_vma=False,
    )
```

time: 320 us -> 120 us (0.38)
  waiting for transfers between devices: 142 us -> 0 us
  Pallas kernels: 0 us -> 113 us
  blocking collectives: 52.7 us -> 0 us
  other arithmetic: 39.5 us -> 0 us
  local copies, waits for them, and re-layouts: 41.4 us -> 6.05 us
  matrix products: 26 us -> 0 us
  between operations: 13.7 us -> 0.03 us
    pallas_call x0 -> x2, Pallas kernels: none -> 113 us  [the longest x1 69.3 us: run_layer(): pl.pallas_call(functools.partial(layer_kernel, n, groups), out_shape=jax....]
    psum x1 -> x0, waiting for transfers between devices: 99 us -> none  [per_device(): lax.psum(jnp.dot(inner, w_out, preferred_element_type=jnp.float32), 'tp')]
    all_to_all x2 -> x0, blocking collectives: 52.7 us -> none  [the longest x1 32.7 us: per_device(): lax.all_to_all(found, 'seq', split_axis=0, concat_axis=0, tiled=True)]
    all_gather x1 -> x0, waiting for transfers between devices: 34 us -> none  [per_device(): gathered = lax.all_gather(own_rows, 'tp', axis=1, tiled=True)]
    another operation x2 -> x0, other arithmetic: 31.1 us -> none
    dot_general x7 -> x0, matrix products: 26 us -> none  [the longest x1 8.79 us: per_device(): jnp.dot(inner, w_out, preferred_element_type=jnp.float32)]
    gather x2 -> x0, local copies, waits for them, and re-layouts: 19.7 us -> none  [the longest x1 10.7 us: per_device(): own_rows = answered[owner, rank]]
    ppermute x1 -> x0, waiting for transfers between devices: 9.3 us -> none  [shifted(): return lax.ppermute(x, axis, pairs)]
  transfers between devices with their start and end apart: 3 -> 0, of which waited for: 3 -> 0; matrix products, arithmetic and copies ran while one was open for 2% -> 0% of each run, Pallas kernels for 0% -> 0%
where the time goes in v1:
time: 120 us; the launch traced here: 119 us
  Pallas kernels  113 us (94%)
  local copies, waits for them, and re-layouts  6.05 us (5%)
    pallas_call x1, Pallas kernels, run_layer(): pl.pallas_call(functools.partial(layer_kernel, n, groups), out_shape=jax....  69.3 us
    pallas_call x1, Pallas kernels, fetch_rows(): pl.pallas_call(functools.partial(rows_kernel, n, plane, cap), out_shape=j...  43.8 us
    unnamed x9, local copies, waits for them, and re-layouts  6.05 us

profile of v1, /device:TPU:32, one launch (start us, length us, event | category | flops | bytes accessed | tf_op | source)
XLA Modules:
  0.0 119.2 jit_solution(10484032949431323327)
XLA Ops:
  0.0 43.8 %shard_map.73 = bf16[1024,256]{1,0:T(8,128)(2,1)} custom-call(s32[1,1024]{1,0:T(1,128)} %bitcast.3, bf16[2048,256]{1,0:T(8,128)(2,1)} %vocab_ref.1), custom_call_target="tpu_custom_call" | custom-call | tf_op jit(solution)/shard_map/pallas_call | solution.py:181
  43.8 0.0 copy-start
  43.8 1.6 %copy-done = bf16[1024,1024]{1,0:T(8,128)(2,1)S(1)} copy-done((bf16[1024,1024]{1,0:T(8,128)(2,1)S(1)}, bf16[1024,1024]{1,0:T(8,128)(2,1)}, u32[]{:S(2)}) %copy-start) | copy-done | bytes 2097176
  45.4 0.0 copy-start.1
  45.4 1.6 %copy-done.1 = bf16[1024,1024]{1,0:T(8,128)(2,1)S(1)} copy-done((bf16[1024,1024]{1,0:T(8,128)(2,1)S(1)}, bf16[1024,1024]{1,0:T(8,128)(2,1)}, u32[]{:S(2)}) %copy-start.1) | copy-done | bytes 2097176
  47.0 0.0 copy-start.2
  47.0 1.0 copy-done.2
  48.1 0.0 copy-start.3
  48.1 1.0 copy-done.3
  49.1 69.3 %shard_map.74 = bf16[256,1024]{1,0:T(8,128)(2,1)S(1)} custom-call(bf16[4,256,256]{2,1,0:T(8,128)(2,1)S(1)} %bitcast.2, bf16[256,1024]{1,0:T(8,128)(2,1)S(1)} %copy-done.3, bf16[1024,1024]{1,0:T(8,128)(2,1)S(1)} %copy-done, bf16[1024,1024]{1,0:T(8,128)(2,1)S(1)} %copy-done.1, bf16[1024,1024]{1,0:T(8,128)(2,1)} %wk_hbm.1, bf16[1024,1024]{1,0:T(8,128)(2,1)} %wv_hbm.1), custom_call_target="tpu_custom_call" | custom-call | tf_op jit(solution)/shard_map/pallas_call | solution.py:420
  118.5 0.8 copy.9
Async XLA Ops:
  43.8 1.6 %copy-start = (bf16[1024,1024]{1,0:T(8,128)(2,1)S(1)}, bf16[1024,1024]{1,0:T(8,128)(2,1)}, u32[]{:S(2)}) copy-start(bf16[1024,1024]{1,0:T(8,128)(2,1)} %win_hbm.1) | copy-start | bytes 6291460
  45.4 1.6 %copy-start.1 = (bf16[1024,1024]{1,0:T(8,128)(2,1)S(1)}, bf16[1024,1024]{1,0:T(8,128)(2,1)}, u32[]{:S(2)}) copy-start(bf16[1024,1024]{1,0:T(8,128)(2,1)} %wout_hbm.1) | copy-start | bytes 6291460
  47.0 1.0 copy-start.2
  48.1 1.0 copy-start.3

commit v2 on v0

v2 whole, which is shorter than its diff:
```python
import functools

import jax
import jax.numpy as jnp
from jax import lax
from jax.experimental import pallas as pl
from jax.experimental.pallas import tpu as pltpu
from jax.sharding import PartitionSpec as P

HEAD_WIDTH = 128
GROUP = 64
F32 = jnp.float32
BF16 = jnp.bfloat16
MESH = pl.DeviceIdType.MESH
PLANE = 8
NT = (((1,), (1,)), ((), ()))


def mm(a, b):
    return jnp.dot(a, b, preferred_element_type=F32)


def layer_kernel(n, groups, plane, cap, ids_ref, vocab_ref, q_ref, win_hbm, wout_hbm, wk_hbm, wv_hbm, out_ref,
                 want, req, sendb, recvb, acc, slots, win, wout, wk, wv, ob, relay_r, relay_l, xb, inner, eb,
                 qnext, wins, head,
                 wsem, isend, irecv, rsend, rrecv, dsend, drecv, ssend, srecv, asend, arecv, es, er, hs, hr):
    tp = 4
    t = lax.axis_index("tp")
    me = lax.axis_index("seq")
    right, left, across = lax.rem(t + 1, tp), lax.rem(t + tp - 1, tp), lax.rem(t + 2, tp)
    ahead, back = lax.rem(me + 1, n), lax.rem(me + n - 1, n)
    planes = n // plane
    mine = me // plane
    rows = ids_ref.shape[1]
    voc, feats = vocab_ref.shape
    block = plane * cap
    shift = voc.bit_length() - 1
    keys = rows // groups
    part = keys // 4
    wide = win.shape[1]
    hidden = win.shape[2]
    width = q_ref.shape[1]
    heads = width // HEAD_WIDTH

    base = (me // 8) * 8
    p = lax.rem(me, 8)
    core = lax.rem(me, 2)
    p_r, p_l, p_x = lax.rem(p + 2, 8), lax.rem(p + 6, 8), lax.rem(p + 4, 8)
    RIGHT, LEFT = {"tp": right}, {"tp": left}
    XR, XL, TWIN = {"seq": base + p_r}, {"seq": base + p_l}, {"seq": me + 1 - 2 * core}
    OTHER = 1 - core

    loads = [
        pltpu.make_async_copy(a, b, wsem.at[i])
        for i, (a, b) in enumerate([(win_hbm, win.at[0]), (wout_hbm, wout.at[0]), (wk_hbm, wk), (wv_hbm, wv)])
    ]
    for load in loads:
        load.start()

    barrier = pltpu.get_barrier_semaphore()

    def step_of(i):
        half = (i + 1) // 2
        return lax.rem(planes // 2 + jnp.where(lax.rem(i, 2) == 1, -half, half) + planes, planes)

    def greet(i, c):
        to = lax.rem(mine + step_of(i), planes)
        for j in range(plane):
            peer = to * plane + j

            @pl.when(peer != me)
            def _():
                pl.semaphore_signal(barrier, inc=1, device_id={"seq": peer}, device_id_type=MESH)

        return c

    lax.fori_loop(0, planes, greet, 0)
    for where in (RIGHT, LEFT):
        pl.semaphore_signal(barrier, inc=1, device_id=where, device_id_type=MESH)

    ids = ids_ref[...]
    owner = ids >> shift
    local = ids & (voc - 1)
    hot = jnp.where(lax.broadcasted_iota(jnp.int32, (n, rows), 0) == owner, 1.0, 0.0).astype(F32)
    hot16 = hot.astype(BF16)
    before = jnp.where(
        lax.broadcasted_iota(jnp.int32, (rows, rows), 0) < lax.broadcasted_iota(jnp.int32, (rows, rows), 1), 1.0, 0.0
    ).astype(BF16)
    count = mm(hot16, before)
    rank = jnp.sum(hot * count, axis=0, keepdims=True).astype(jnp.int32)
    ranked = lax.broadcasted_iota(jnp.int32, (128, rows), 0) == rank
    low = jnp.where(ranked, (local & 255).astype(F32), 0.0).astype(BF16)
    high = jnp.where(ranked, (local >> 8).astype(F32), 0.0).astype(BF16)
    table = lax.dot_general(hot16, low, NT, preferred_element_type=F32) + 256.0 * lax.dot_general(
        hot16, high, NT, preferred_element_type=F32
    )
    table = table.astype(jnp.int32)
    for o in range(n):
        want[o] = table[o : o + 1]

    pl.semaphore_wait(barrier, n - 1 + 2)

    def remote(src, dst, ssem, rsem, where):
        return pltpu.make_async_remote_copy(
            src_ref=src, dst_ref=dst, send_sem=ssem, recv_sem=rsem, device_id=where, device_id_type=MESH
        )

    def ids_copy(peer):
        return remote(want.at[peer], req.at[me], isend.at[peer], irecv.at[me], {"seq": peer})

    def ids_arrival(src):
        return remote(want.at[src], req.at[src], isend.at[src], irecv.at[src], {"seq": src})

    def rows_copy(peer):
        return remote(sendb.at[peer], recvb.at[me], rsend.at[peer], rrecv.at[me], {"seq": peer})

    def rows_arrival(src):
        return remote(sendb.at[src], recvb.at[src], rsend.at[src], rrecv.at[src], {"seq": src})

    def send_ids(i, c):
        to = lax.rem(mine + step_of(i), planes)
        for j in range(plane):
            peer = to * plane + j

            @pl.when(peer != me)
            def _():
                ids_copy(peer).start()

        return c

    lax.fori_loop(0, planes, send_ids, 0)

    quarter = wide // 4

    def a_part(c, k):
        return pl.ds(pl.multiple_of(c * (2 * quarter) + k * quarter, quarter), quarter)

    def a_half(c):
        return pl.ds(pl.multiple_of(c * (2 * quarter), 2 * quarter), 2 * quarter)

    lot = hidden // 8
    lot2 = lot // 2

    def b_lot(i):
        return pl.ds(pl.multiple_of(i * lot, lot), lot)

    def b_half(i, k):
        return pl.ds(pl.multiple_of(i * lot + k * lot2, lot2), lot2)

    in_r = [remote(win_hbm.at[a_part(core, k)], win.at[1, a_part(core, k)], dsend.at[k], drecv.at[k], RIGHT) for k in (0, 1)]
    in_l = [remote(win_hbm.at[a_part(core, k)], win.at[2, a_part(core, k)], dsend.at[2 + k], drecv.at[2 + k], LEFT) for k in (0, 1)]
    eighth = quarter // 2

    def a_sub(c, k, j):
        return pl.ds(pl.multiple_of(c * (2 * quarter) + k * quarter + j * eighth, eighth), eighth)

    def a_on(k, j):
        at = a_sub(core, k, j)
        return remote(win.at[1 + k, at], win.at[3, at], dsend.at[4 + 2 * j + k], drecv.at[4 + 2 * j + k], (RIGHT, LEFT)[k])

    def a_twin(c, k, j):
        at = a_sub(c, k, j)
        return remote(win.at[3, at], win.at[3, at], dsend.at[8 + 2 * j + k], drecv.at[8 + 2 * j + k], TWIN)

    def a_twins(c):
        both = win.at[pl.ds(1, 2), a_half(c)]
        return remote(both, both, dsend.at[12], drecv.at[12], TWIN)

    on = [[a_on(k, j) for k in (0, 1)] for j in (0, 1)]
    twin_3 = [[a_twin(core, k, j) for k in (0, 1)] for j in (0, 1)]
    twin_12 = a_twins(core)
    lot_r = remote(wout_hbm.at[b_lot(p)], wout.at[1, b_lot(p)], ssend.at[0], srecv.at[0], RIGHT)
    lot_l = remote(wout_hbm.at[b_lot(p)], wout.at[2, b_lot(p)], ssend.at[1], srecv.at[1], LEFT)
    lot_on_r = remote(wout.at[1, b_half(p, 0)], wout.at[3, b_half(p, 0)], ssend.at[2], srecv.at[2], RIGHT)
    lot_on_l = remote(wout.at[2, b_half(p, 1)], wout.at[3, b_half(p, 1)], ssend.at[3], srecv.at[3], LEFT)
    slots_of = (pl.ds(1, 2), pl.ds(3, 1))

    def share(m, at, i, where):
        both = wout.at[slots_of[m], at]
        return remote(both, both, ssend.at[4 + 8 * m + i], srecv.at[4 + 8 * m + i], where)

    x_r = [share(m, b_lot(p), 0, XR) for m in (0, 1)]
    x_l = [share(m, b_lot(p), 1, XL) for m in (0, 1)]
    x_on_r = [share(m, b_half(p_l, 0), 2, XR) for m in (0, 1)]
    x_on_l = [share(m, b_half(p_r, 1), 3, XL) for m in (0, 1)]
    twins = [[share(m, b_lot(q), 4 + i, TWIN) for i, q in enumerate((p, p_l, p_r, p_x))] for m in (0, 1)]

    def x_start(m):
        x_r[m].start()
        x_l[m].start()
        twins[m][0].start()

    def x_forward(m):
        x_r[m].wait_recv()
        x_l[m].wait_recv()
        x_on_r[m].start()
        x_on_l[m].start()
        twins[m][1].start()
        twins[m][2].start()

    def x_finish(m):
        x_on_r[m].wait_recv()
        x_on_l[m].wait_recv()
        twins[m][3].start()

    lot_r.start()
    lot_l.start()
    in_r[0].start()
    in_l[1].start()
    q_back = remote(q_ref.at[pl.ds(0, GROUP)], qnext, hs.at[0], hr.at[0], {"seq": back})
    q_back.start()
    req[me] = want[me]

    slot = (owner * cap + rank).astype(F32)
    slots[...] = jnp.transpose(jnp.broadcast_to(slot, (128, rows)))

    def answer(i, c):
        to = lax.rem(mine + step_of(i), planes)
        for j in range(plane):
            peer = to * plane + j

            @pl.when(peer != me)
            def _():
                ids_arrival(peer).wait_recv()

        @pl.when(i == 2)
        def _():
            lot_r.wait_recv()
            lot_on_r.start()
            lot_l.wait_recv()
            lot_on_l.start()
            x_start(0)
            in_r[1].start()
            in_l[0].start()

        asked = jnp.concatenate([req[to * plane + j] for j in range(plane)], axis=0).astype(F32)
        asked = jnp.transpose(jnp.concatenate([asked, jnp.zeros((128 - plane, 128), F32)], axis=0))
        cols = [jnp.broadcast_to(asked[:cap, j : j + 1], (cap, 128)) for j in range(plane)]
        col = jnp.concatenate(cols, axis=0)
        total = jnp.zeros((block, feats), F32)
        deep = min(256, voc)
        for v in range(0, voc, deep):
            picks = [
                jnp.where(
                    col == (lax.broadcasted_iota(jnp.int32, (block, 128), 1) + (v + w)).astype(F32), 1.0, 0.0
                ).astype(BF16)
                for w in range(0, deep, 128)
            ]
            total += mm(jnp.concatenate(picks, axis=1), vocab_ref[v : v + deep, :])
        found = total.astype(BF16)
        for j in range(plane):
            sendb[to * plane + j] = found[j * cap : (j + 1) * cap]
        for j in range(plane):
            peer = to * plane + j

            @pl.when(peer != me)
            def _():
                rows_copy(peer).start()

        return c

    lax.fori_loop(0, planes, answer, 0)
    recvb[me] = sendb[me]

    acc[...] = jnp.zeros_like(acc)

    def gather(i, c):
        @pl.when(i == 1)
        def _():
            in_r[0].wait_recv()
            on[0][0].start()
            on[1][0].start()
            in_l[1].wait_recv()
            on[0][1].start()
            on[1][1].start()

        @pl.when(i == 2)
        def _():
            lot_on_r.wait_recv()
            lot_on_l.wait_recv()
            x_start(1)

        @pl.when(i == 3)
        def _():
            x_forward(0)

        @pl.when(i == 5)
        def _():
            x_finish(0)
            x_forward(1)

        @pl.when(i == 6)
        def _():
            in_r[1].wait_recv()
            in_l[0].wait_recv()
            twin_12.start()

        @pl.when(i == 7)
        def _():
            x_finish(1)

        source = lax.rem(mine - step_of(i) + planes, planes)
        for j in range(plane):
            src = source * plane + j

            @pl.when(src != me)
            def _():
                rows_arrival(src).wait_recv()

        first = (source * block).astype(F32)
        at = slots[...] - first
        picks = [
            jnp.where(at == (lax.broadcasted_iota(jnp.int32, (rows, 128), 1) + w).astype(F32), 1.0, 0.0).astype(BF16)
            for w in range(0, block, 128)
        ]
        got = jnp.concatenate([recvb[source * plane + j] for j in range(plane)], axis=0)
        acc[...] += mm(jnp.concatenate(picks, axis=1), got)
        return c

    lax.fori_loop(0, planes, gather, 0)

    ob[...] = acc[...].reshape(groups, 4, part, feats).astype(BF16)
    low_part, high_part = pl.ds(0, part // 2), pl.ds(part // 2, part // 2)
    hop_r = remote(ob.at[:, across, low_part], relay_r, asend.at[0], arecv.at[0], RIGHT)
    hop_l = remote(ob.at[:, across, high_part], relay_l, asend.at[1], arecv.at[1], LEFT)
    give_r = remote(ob.at[:, right], xb.at[1], asend.at[2], arecv.at[2], RIGHT)
    give_l = remote(ob.at[:, left], xb.at[2], asend.at[3], arecv.at[3], LEFT)
    far_r = remote(relay_r, xb.at[3, :, low_part], asend.at[4], arecv.at[4], RIGHT)
    far_l = remote(relay_l, xb.at[3, :, high_part], asend.at[5], arecv.at[5], LEFT)
    hop_r.start()
    hop_l.start()
    give_r.start()
    give_l.start()
    xb[0] = ob[:, t]
    hop_r.wait_recv()
    far_r.start()
    hop_l.wait_recv()
    far_l.start()
    for j in (0, 1):
        for k in (0, 1):
            on[j][k].wait_recv()
            twin_3[j][k].start()
    for copy in (give_r, give_l, far_r, far_l):
        copy.wait_recv()

    slices = [t, left, right, across]

    def feature(i):
        return pl.ds(pl.multiple_of(slices[i] * feats, feats), feats)

    square = jnp.zeros((keys, 1), F32)
    for i in range(4):
        v = xb[i].reshape(keys, feats).astype(F32)
        square += jnp.sum(v * v, axis=-1, keepdims=True)
    scale = lax.rsqrt(square * (1.0 / wide) + 1e-06)
    normed = [(xb[i].reshape(keys, feats).astype(F32) * scale).astype(BF16) for i in range(4)]

    def twin_arrival(i):
        if i == 1:
            a_twins(OTHER).wait_recv()
        if i == 3:
            for j in (0, 1):
                for k in (0, 1):
                    a_twin(OTHER, k, j).wait_recv()

    loads[0].wait()
    for i in range(4):
        twin_arrival(i)
        hid = jnp.zeros((keys, hidden), F32)
        for f in range(4):
            hid += mm(normed[f], win[i, feature(f), :])
        inner[i] = jax.nn.gelu(hid, approximate=True).astype(BF16)
    loads[1].wait()
    for i, q in enumerate((p, p_l, p_r, p_x)):
        for m in (0, 1):
            share(m, b_lot(q + 1 - 2 * core), 4 + i, TWIN).wait_recv()
    for f in range(4):
        total = xb[f].reshape(keys, feats).astype(F32)
        for i in range(4):
            total += mm(inner[i], wout[i, :, feature(f)])
        total = total.astype(BF16)
        for g in range(groups):
            eb[g, 0, :, feature(f)] = total[g * part : (g + 1) * part]

    def ring(g):
        own = eb.at[g, 0]
        return dict(
            own_r=remote(own, eb.at[g, 1], es.at[g, 0], er.at[g, 0], RIGHT),
            own_l=remote(own, eb.at[g, 2], es.at[g, 1], er.at[g, 1], LEFT),
            fwd_r=remote(eb.at[g, 1, low_part], eb.at[g, 3, low_part], es.at[g, 2], er.at[g, 2], RIGHT),
            fwd_l=remote(eb.at[g, 2, high_part], eb.at[g, 3, high_part], es.at[g, 3], er.at[g, 3], LEFT),
        )

    table_e = [ring(g) for g in range(groups)]
    head_on = remote(wins.at[groups], head, hs.at[1], hr.at[1], {"seq": ahead})
    soft = HEAD_WIDTH ** (-0.5)

    def shifted(rows_a, by):
        pick = lax.broadcasted_iota(jnp.int32, (GROUP, 2 * GROUP), 1) == (
            lax.broadcasted_iota(jnp.int32, (GROUP, 2 * GROUP), 0) + by
        )
        return mm(jnp.where(pick, 1.0, 0.0).astype(BF16), rows_a).astype(BF16)

    def attend(g):
        table_e[g]["fwd_r"].wait_recv()
        table_e[g]["fwd_l"].wait_recv()
        enc = eb[g].reshape(keys, wide)
        kk = mm(enc, wk[...]).astype(BF16)
        vv = mm(enc, wv[...]).astype(BF16)
        if g == groups - 1:
            q_back.wait_recv()
            both = jnp.concatenate([q_ref[g * GROUP : (g + 1) * GROUP, :], qnext[...]], axis=0)
        else:
            both = q_ref[g * GROUP : (g + 2) * GROUP, :]
        qg = shifted(both, GROUP - 1)
        for h in range(heads):
            at = slice(h * HEAD_WIDTH, (h + 1) * HEAD_WIDTH)
            logits = lax.dot_general(qg[:, at], kk[:, at], NT, preferred_element_type=F32) * soft
            expo = jnp.exp(logits)
            probs = (expo * (1.0 / jnp.sum(expo, axis=-1, keepdims=True))).astype(BF16)
            wins[g + 1, :, at] = mm(probs, vv[:, at]).astype(BF16)

    order = [groups - 1] + list(range(groups - 1))

    def own_out(k):
        table_e[order[k]]["own_r"].start()
        table_e[order[k]]["own_l"].start()

    def onward(k):
        c = table_e[order[k]]
        c["own_r"].wait_recv()
        c["fwd_r"].start()
        c["own_l"].wait_recv()
        c["fwd_l"].start()

    own_out(0)
    own_out(1)
    loads[2].wait()
    loads[3].wait()
    onward(0)
    own_out(2)
    onward(1)
    own_out(3)
    attend(order[0])
    head_on.start()
    onward(2)
    attend(order[1])
    onward(3)
    attend(order[2])
    head_on.wait_recv()
    at_start = jnp.where(me == 0, 0.0, 1.0)
    wins[0] = jnp.where(at_start > 0.0, head[...].astype(F32), 0.0).astype(BF16)
    attend(order[3])
    for b in range(groups):
        both = jnp.concatenate([wins[b], wins[b + 1]], axis=0)
        out_ref[b * GROUP : (b + 1) * GROUP, :] = shifted(both, 1)

    def drain(k, c):
        peer = lax.rem(me + k, n)
        ids_copy(peer).wait_send()
        rows_copy(peer).wait_send()
        return c

    lax.fori_loop(1, n, drain, 0)
    for g in range(groups):
        for copy in table_e[g].values():
            copy.wait_send()
    for copy in in_r + in_l + on[0] + on[1] + twin_3[0] + twin_3[1] + twins[0] + twins[1] + x_r + x_l + x_on_r + x_on_l + [
        twin_12, lot_r, lot_l, lot_on_r, lot_on_l,
        hop_r, hop_l, give_r, give_l, far_r, far_l, q_back, head_on,
    ]:
        copy.wait_send()


def per_device(n, queries, vocab_rows, neighbour_ids, w_in, w_out, w_key, w_value):
    groups = neighbour_ids.shape[0]
    ids = neighbour_ids.reshape(1, -1)
    rows = ids.shape[1]
    cap = 2 * rows // n
    plane = PLANE
    feats = vocab_rows.shape[1]
    tok, width = queries.shape
    wide, hidden = w_in.shape
    keys = rows // groups
    part = keys // 4
    vm = lambda shape, dt=BF16: pltpu.VMEM(shape, dt)
    dma = pltpu.SemaphoreType.DMA
    return pl.pallas_call(
        functools.partial(layer_kernel, n, groups, plane, cap),
        out_shape=jax.ShapeDtypeStruct((tok, width), BF16),
        in_specs=[pl.BlockSpec(memory_space=pltpu.VMEM)] * 3 + [pl.BlockSpec(memory_space=pltpu.MemorySpace.HBM)] * 4,
        out_specs=pl.BlockSpec(memory_space=pltpu.VMEM),
        scratch_shapes=[
            vm((n, 1, 128), jnp.int32), vm((n, 1, 128), jnp.int32),
            vm((n, cap, feats)), vm((n, cap, feats)), vm((rows, feats), F32), vm((rows, 128), F32),
            vm((4, wide, hidden)), vm((4, hidden, wide)), vm(w_key.shape), vm(w_value.shape),
            vm((groups, 4, part, feats)),
            vm((groups, part // 2, feats)), vm((groups, part // 2, feats)),
            vm((4, groups, part, feats)), vm((4, keys, hidden)), vm((groups, 4, part, wide)),
            vm((GROUP, width)), vm((groups + 1, GROUP, width)), vm((GROUP, width)),
            dma((4,)), dma((n,)), dma((n,)), dma((n,)), dma((n,)),
            dma((13,)), dma((13,)), dma((20,)), dma((20,)), dma((6,)), dma((6,)),
            dma((groups, 4)), dma((groups, 4)), dma((2,)), dma((2,)),
        ],
        compiler_params=pltpu.CompilerParams(
            collective_id=0, has_side_effects=True, vmem_limit_bytes=58 * 1024 * 1024
        ),
    )(ids, vocab_rows, queries, w_in, w_out, w_key, w_value)


def solution(mesh):
    return jax.shard_map(
        functools.partial(per_device, mesh.shape["seq"]),
        mesh=mesh,
        in_specs=(
            P("seq", "tp"),
            P("seq", "tp"),
            P("seq", None, None),
            P(None, "tp"),
            P("tp", None),
            P(None, "tp"),
            P(None, "tp"),
        ),
        out_specs=P("seq", "tp"),
        check_vma=False,
    )
```

time: 320 us -> 106 us (0.33)
  waiting for transfers between devices: 142 us -> 0 us
  Pallas kernels: 0 us -> 104 us
  blocking collectives: 52.7 us -> 0 us
  local copies, waits for them, and re-layouts: 41.4 us -> 1.87 us
  other arithmetic: 39.5 us -> 0 us
  matrix products: 26 us -> 0 us
  between operations: 13.7 us -> 0.01 us
    pallas_call x0 -> x1, Pallas kernels: none -> 104 us  [per_device(): pl.pallas_call(functools.partial(layer_kernel, n, groups, plane, cap), ou...]
    psum x1 -> x0, waiting for transfers between devices: 99 us -> none  [per_device(): lax.psum(jnp.dot(inner, w_out, preferred_element_type=jnp.float32), 'tp')]
    all_to_all x2 -> x0, blocking collectives: 52.7 us -> none  [the longest x1 32.7 us: per_device(): lax.all_to_all(found, 'seq', split_axis=0, concat_axis=0, tiled=True)]
    all_gather x1 -> x0, waiting for transfers between devices: 34 us -> none  [per_device(): gathered = lax.all_gather(own_rows, 'tp', axis=1, tiled=True)]
    another operation x2 -> x0, other arithmetic: 31.1 us -> none
    dot_general x7 -> x0, matrix products: 26 us -> none  [the longest x1 8.79 us: per_device(): jnp.dot(inner, w_out, preferred_element_type=jnp.float32)]
    gather x2 -> x0, local copies, waits for them, and re-layouts: 19.7 us -> none  [the longest x1 10.7 us: per_device(): own_rows = answered[owner, rank]]
    ppermute x1 -> x0, waiting for transfers between devices: 9.3 us -> none  [shifted(): return lax.ppermute(x, axis, pairs)]
  transfers between devices with their start and end apart: 3 -> 0, of which waited for: 3 -> 0; matrix products, arithmetic and copies ran while one was open for 2% -> 0% of each run, Pallas kernels for 0% -> 0%
where the time goes in v2:
time: 106 us
  Pallas kernels  104 us (98%)
  local copies, waits for them, and re-layouts  1.87 us (2%)
    pallas_call x1, Pallas kernels, per_device(): pl.pallas_call(functools.partial(layer_kernel, n, groups, plane, cap), ou...  104 us

profile of v2, /device:TPU:32, one launch (start us, length us, event | category | flops | bytes accessed | tf_op | source)
XLA Modules:
  0.0 105.9 jit_solution(14026019306985038828)
XLA Ops:
  0.0 104.0 %shard_map.73 = bf16[256,1024]{1,0:T(8,128)(2,1)} custom-call(s32[1,1024]{1,0:T(1,128)} %bitcast.1, bf16[2048,256]{1,0:T(8,128)(2,1)} %vocab_ref.1, bf16[256,1024]{1,0:T(8,128)(2,1)} %q_ref.1, bf16[1024,1024]{1,0:T(8,128)(2,1)} %win_hbm.1, bf16[1024,1024]{1,0:T(8,128)(2,1)} %wout_hbm.1, bf16[1024,1024]{1,0:T(8,128)(2,1)} %wk_hbm.1, bf16[1024,1024]{1,0:T(8,128)(2,1)} %wv_hbm.1), custom_call_target="tpu_custom_call" | custom-call | tf_op jit(solution)/shard_map/pallas_call | solution.py:488
  104.0 1.9 %copy.9 = bf16[256,1024]{1,0:T(8,128)(2,1)} copy(bf16[256,1024]{1,0:T(8,128)(2,1)} %shard_map.73) | data formatting | bytes 1048576

commit v3 on v2

--- a/solution.py
+++ b/solution.py
@@ -20,9 +20,9 @@
     return jnp.dot(a, b, preferred_element_type=F32)
 
 
-def layer_kernel(n, groups, plane, cap, ids_ref, vocab_ref, q_ref, win_hbm, wout_hbm, wk_hbm, wv_hbm, out_ref,
+def layer_kernel(n, groups, plane, cap, ids_ref, vocab_ref, q_ref, win_hbm, wout_hbm, wk_hbm, wv_hbm, wins,
                  want, req, sendb, recvb, acc, slots, win, wout, wk, wv, ob, relay_r, relay_l, xb, inner, eb,
-                 qnext, wins, head,
+                 qnext, head,
                  wsem, isend, irecv, rsend, rrecv, dsend, drecv, ssend, srecv, asend, arecv, es, er, hs, hr):
     tp = 4
     t = lax.axis_index("tp")
@@ -280,24 +280,15 @@
             lot_on_l.wait_recv()
             x_start(1)
 
-        @pl.when(i == 3)
+        @pl.when(i == 5)
         def _():
             x_forward(0)
-
-        @pl.when(i == 5)
-        def _():
-            x_finish(0)
-            x_forward(1)
 
         @pl.when(i == 6)
         def _():
             in_r[1].wait_recv()
             in_l[0].wait_recv()
             twin_12.start()
-
-        @pl.when(i == 7)
-        def _():
-            x_finish(1)
 
         source = lax.rem(mine - step_of(i) + planes, planes)
         for j in range(plane):
@@ -332,6 +323,7 @@
     give_r.start()
     give_l.start()
     xb[0] = ob[:, t]
+    x_forward(1)
     hop_r.wait_recv()
     far_r.start()
     hop_l.wait_recv()
@@ -340,6 +332,7 @@
         for k in (0, 1):
             on[j][k].wait_recv()
             twin_3[j][k].start()
+    x_finish(0)
     for copy in (give_r, give_l, far_r, far_l):
         copy.wait_recv()
 
@@ -365,6 +358,8 @@
 
     loads[0].wait()
     for i in range(4):
+        if i == 2:
+            x_finish(1)
         twin_arrival(i)
         hid = jnp.zeros((keys, hidden), F32)
         for f in range(4):
@@ -451,9 +446,6 @@
     at_start = jnp.where(me == 0, 0.0, 1.0)
     wins[0] = jnp.where(at_start > 0.0, head[...].astype(F32), 0.0).astype(BF16)
     attend(order[3])
-    for b in range(groups):
-        both = jnp.concatenate([wins[b], wins[b + 1]], axis=0)
-        out_ref[b * GROUP : (b + 1) * GROUP, :] = shifted(both, 1)
 
     def drain(k, c):
         peer = lax.rem(me + k, n)
@@ -485,9 +477,9 @@
     part = keys // 4
     vm = lambda shape, dt=BF16: pltpu.VMEM(shape, dt)
     dma = pltpu.SemaphoreType.DMA
-    return pl.pallas_call(
+    windows = pl.pallas_call(
         functools.partial(layer_kernel, n, groups, plane, cap),
-        out_shape=jax.ShapeDtypeStruct((tok, width), BF16),
+        out_shape=jax.ShapeDtypeStruct((groups + 1, GROUP, width), BF16),
         in_specs=[pl.BlockSpec(memory_space=pltpu.VMEM)] * 3 + [pl.BlockSpec(memory_space=pltpu.MemorySpace.HBM)] * 4,
         out_specs=pl.BlockSpec(memory_space=pltpu.VMEM),
         scratch_shapes=[
@@ -497,7 +489,7 @@
             vm((groups, 4, part, feats)),
             vm((groups, part // 2, feats)), vm((groups, part // 2, feats)),
             vm((4, groups, part, feats)), vm((4, keys, hidden)), vm((groups, 4, part, wide)),
-            vm((GROUP, width)), vm((groups + 1, GROUP, width)), vm((GROUP, width)),
+            vm((GROUP, width)), vm((GROUP, width)),
             dma((4,)), dma((n,)), dma((n,)), dma((n,)), dma((n,)),
             dma((13,)), dma((13,)), dma((20,)), dma((20,)), dma((6,)), dma((6,)),
             dma((groups, 4)), dma((groups, 4)), dma((2,)), dma((2,)),
@@ -506,6 +498,7 @@
             collective_id=0, has_side_effects=True, vmem_limit_bytes=58 * 1024 * 1024
         ),
     )(ids, vocab_rows, queries, w_in, w_out, w_key, w_value)
+    return windows.reshape((groups + 1) * GROUP, width)[1 : 1 + tok]
 
 
 def solution(mesh):

time: 106 us -> 102 us (0.962)
  Pallas kernels: 104 us -> 99.3 us
    pallas_call x1, Pallas kernels: 104 us -> 99.3 us  [per_device(): pl.pallas_call(functools.partial(layer_kernel, n, groups, plane, cap), ou...]
    slice x0 -> x1, local copies, waits for them, and re-layouts: none -> 1.97 us  [per_device(): return windows.reshape((groups + 1) * GROUP, width)[1:1 + tok]]
    unnamed x1 -> x0, local copies, waits for them, and re-layouts: 1.87 us -> none
where the time goes in v3:
time: 102 us; the launch traced here: 101 us
  Pallas kernels  99.3 us (97%)
  local copies, waits for them, and re-layouts  1.97 us (2%)
    pallas_call x1, Pallas kernels, per_device(): pl.pallas_call(functools.partial(layer_kernel, n, groups, plane, cap), ou...  99.3 us

profile of v3, /device:TPU:32, one launch (start us, length us, event | category | flops | bytes accessed | tf_op | source)
XLA Modules:
  0.0 101.3 jit_solution(17649093814373026881)
XLA Ops:
  0.0 99.3 %shard_map.73 = bf16[5,64,1024]{2,1,0:T(8,128)(2,1)} custom-call(s32[1,1024]{1,0:T(1,128)} %bitcast.3, bf16[2048,256]{1,0:T(8,128)(2,1)} %vocab_ref.1, bf16[256,1024]{1,0:T(8,128)(2,1)} %q_ref.1, bf16[1024,1024]{1,0:T(8,128)(2,1)} %win_hbm.1, bf16[1024,1024]{1,0:T(8,128)(2,1)} %wout_hbm.1, bf16[1024,1024]{1,0:T(8,128)(2,1)} %wk_hbm.1, bf16[1024,1024]{1,0:T(8,128)(2,1)} %wv_hbm.1), custom_call_target="tpu_custom_call" | custom-call | tf_op jit(solution)/shard_map/pallas_call | solution.py:480
  99.3 2.0 %slice.4 = bf16[256,1024]{1,0:T(8,128)(2,1)} slice(bf16[320,1024]{1,0:T(8,128)(2,1)} %bitcast.2), slice={[1:257], [0:1024]} | slice | bytes 1048576 | tf_op jit(solution)/shard_map/slice | solution.py:501

commit v4 on v3

--- a/solution.py
+++ b/solution.py
@@ -23,7 +23,7 @@
 def layer_kernel(n, groups, plane, cap, ids_ref, vocab_ref, q_ref, win_hbm, wout_hbm, wk_hbm, wv_hbm, wins,
                  want, req, sendb, recvb, acc, slots, win, wout, wk, wv, ob, relay_r, relay_l, xb, inner, eb,
                  qnext, head,
-                 wsem, isend, irecv, rsend, rrecv, dsend, drecv, ssend, srecv, asend, arecv, es, er, hs, hr):
+                 wsem, isend, irecv, rsend, rrecv, dsend, drecv, ssend, srecv, asend, arecv, es, er, hs, hr, spread):
     tp = 4
     t = lax.axis_index("tp")
     me = lax.axis_index("seq")
@@ -63,21 +63,127 @@
         half = (i + 1) // 2
         return lax.rem(planes // 2 + jnp.where(lax.rem(i, 2) == 1, -half, half) + planes, planes)
 
-    def greet(i, c):
+    depth = n // 8
+    up, down = {"seq": lax.rem(me + 8, n)}, {"seq": lax.rem(me + n - 8, n)}
+    near = [RIGHT, LEFT, XR, XL, TWIN] + ([up, down] if depth > 2 else [])
+    for where in near:
+        pl.semaphore_signal(barrier, inc=1, device_id=where, device_id_type=MESH)
+
+    pl.semaphore_wait(barrier, len(near))
+
+    def remote(src, dst, ssem, rsem, where):
+        return pltpu.make_async_remote_copy(
+            src_ref=src, dst_ref=dst, send_sem=ssem, recv_sem=rsem, device_id=where, device_id_type=MESH
+        )
+
+    def ids_copy(peer):
+        return remote(want.at[peer], req.at[me], isend.at[peer], irecv.at[me], {"seq": peer})
+
+    def ids_arrival(src):
+        return remote(want.at[src], req.at[src], isend.at[src], irecv.at[src], {"seq": src})
+
+    def rows_copy(peer):
+        return remote(sendb.at[peer], recvb.at[me], rsend.at[peer], rrecv.at[me], {"seq": peer})
+
+    def rows_arrival(src):
+        return remote(sendb.at[src], recvb.at[src], rsend.at[src], rrecv.at[src], {"seq": src})
+
+    def send_ids(i, c):
         to = lax.rem(mine + step_of(i), planes)
         for j in range(plane):
             peer = to * plane + j
 
             @pl.when(peer != me)
             def _():
-                pl.semaphore_signal(barrier, inc=1, device_id={"seq": peer}, device_id_type=MESH)
+                ids_copy(peer).start()
 
         return c
 
-    lax.fori_loop(0, planes, greet, 0)
-    for where in (RIGHT, LEFT):
-        pl.semaphore_signal(barrier, inc=1, device_id=where, device_id_type=MESH)
-
+    quarter = wide // 4
+
+    def a_part(c, k):
+        return pl.ds(pl.multiple_of(c * (2 * quarter) + k * quarter, quarter), quarter)
+
+    def a_half(c):
+        return pl.ds(pl.multiple_of(c * (2 * quarter), 2 * quarter), 2 * quarter)
+
+    lot = hidden // 8
+    lot2 = lot // 2
+
+    def b_lot(i):
+        return pl.ds(pl.multiple_of(i * lot, lot), lot)
+
+    def b_half(i, k):
+        return pl.ds(pl.multiple_of(i * lot + k * lot2, lot2), lot2)
+
+    in_r = [remote(win_hbm.at[a_part(core, k)], win.at[1, a_part(core, k)], dsend.at[k], drecv.at[k], RIGHT) for k in (0, 1)]
+    in_l = [remote(win_hbm.at[a_part(core, k)], win.at[2, a_part(core, k)], dsend.at[2 + k], drecv.at[2 + k], LEFT) for k in (0, 1)]
+    eighth = quarter // 2
+
+    def a_sub(c, k, j):
+        return pl.ds(pl.multiple_of(c * (2 * quarter) + k * quarter + j * eighth, eighth), eighth)
+
+    def a_on(k, j):
+        at = a_sub(core, k, j)
+        return remote(win.at[1 + k, at], win.at[3, at], dsend.at[4 + 2 * j + k], drecv.at[4 + 2 * j + k], (RIGHT, LEFT)[k])
+
+    def a_twin(c, k, j):
+        at = a_sub(c, k, j)
+        return remote(win.at[3, at], win.at[3, at], dsend.at[8 + 2 * j + k], drecv.at[8 + 2 * j + k], TWIN)
+
+    def a_twins(c):
+        both = win.at[pl.ds(1, 2), a_half(c)]
+        return remote(both, both, dsend.at[12], drecv.at[12], TWIN)
+
+    on = [[a_on(k, j) for k in (0, 1)] for j in (0, 1)]
+    twin_3 = [[a_twin(core, k, j) for k in (0, 1)] for j in (0, 1)]
+    twin_12 = a_twins(core)
+    lot_r = remote(wout_hbm.at[b_lot(p)], wout.at[1, b_lot(p)], ssend.at[0], srecv.at[0], RIGHT)
+    lot_l = remote(wout_hbm.at[b_lot(p)], wout.at[2, b_lot(p)], ssend.at[1], srecv.at[1], LEFT)
+    lot_on_r = remote(wout.at[1, b_half(p, 0)], wout.at[3, b_half(p, 0)], ssend.at[2], srecv.at[2], RIGHT)
+    lot_on_l = remote(wout.at[2, b_half(p, 1)], wout.at[3, b_half(p, 1)], ssend.at[3], srecv.at[3], LEFT)
+    slots_of = (pl.ds(1, 2), pl.ds(3, 1))
+
+    def share(m, at, i, where):
+        both = wout.at[slots_of[m], at]
+        return remote(both, both, ssend.at[4 + 8 * m + i], srecv.at[4 + 8 * m + i], where)
+
+    x_r = [share(m, b_lot(p), 0, XR) for m in (0, 1)]
+    x_l = [share(m, b_lot(p), 1, XL) for m in (0, 1)]
+    x_on_r = [share(m, b_half(p_l, 0), 2, XR) for m in (0, 1)]
+    x_on_l = [share(m, b_half(p_r, 1), 3, XL) for m in (0, 1)]
+    twins = [[share(m, b_lot(q), 4 + i, TWIN) for i, q in enumerate((p, p_l, p_r, p_x))] for m in (0, 1)]
+
+    def x_start(m):
+        x_r[m].start()
+        x_l[m].start()
+        twins[m][0].start()
+
+    def x_forward(m):
+        x_r[m].wait_recv()
+        x_l[m].wait_recv()
+        x_on_r[m].start()
+        x_on_l[m].start()
+        twins[m][1].start()
+        twins[m][2].start()
+
+    def x_finish(m):
+        x_on_r[m].wait_recv()
+        x_on_l[m].wait_recv()
+        twins[m][3].start()
+
+    lot_r.start()
+    lot_l.start()
+    in_r[0].start()
+    in_l[1].start()
+    q_back = remote(q_ref.at[pl.ds(0, GROUP)], qnext, hs.at[0], hr.at[0], {"seq": back})
+    def tell(i, where):
+        pl.semaphore_signal(spread.at[i], inc=1, device_id=where, device_id_type=MESH)
+
+    def heard(i):
+        pl.semaphore_wait(spread.at[i], 1)
+
+    tell(0, TWIN)
     ids = ids_ref[...]
     owner = ids >> shift
     local = ids & (voc - 1)
@@ -88,131 +194,39 @@
     ).astype(BF16)
     count = mm(hot16, before)
     rank = jnp.sum(hot * count, axis=0, keepdims=True).astype(jnp.int32)
+    heard(0)
+    tell(1, XR)
+    tell(2, XL)
     ranked = lax.broadcasted_iota(jnp.int32, (128, rows), 0) == rank
     low = jnp.where(ranked, (local & 255).astype(F32), 0.0).astype(BF16)
     high = jnp.where(ranked, (local >> 8).astype(F32), 0.0).astype(BF16)
     table = lax.dot_general(hot16, low, NT, preferred_element_type=F32) + 256.0 * lax.dot_general(
         hot16, high, NT, preferred_element_type=F32
     )
+    heard(1)
+    heard(2)
+    tell(3, XR)
     table = table.astype(jnp.int32)
     for o in range(n):
         want[o] = table[o : o + 1]
 
-    pl.semaphore_wait(barrier, n - 1 + 2)
-
-    def remote(src, dst, ssem, rsem, where):
-        return pltpu.make_async_remote_copy(
-            src_ref=src, dst_ref=dst, send_sem=ssem, recv_sem=rsem, device_id=where, device_id_type=MESH
-        )
-
-    def ids_copy(peer):
-        return remote(want.at[peer], req.at[me], isend.at[peer], irecv.at[me], {"seq": peer})
-
-    def ids_arrival(src):
-        return remote(want.at[src], req.at[src], isend.at[src], irecv.at[src], {"seq": src})
-
-    def rows_copy(peer):
-        return remote(sendb.at[peer], recvb.at[me], rsend.at[peer], rrecv.at[me], {"seq": peer})
-
-    def rows_arrival(src):
-        return remote(sendb.at[src], recvb.at[src], rsend.at[src], rrecv.at[src], {"seq": src})
-
-    def send_ids(i, c):
-        to = lax.rem(mine + step_of(i), planes)
-        for j in range(plane):
-            peer = to * plane + j
-
-            @pl.when(peer != me)
-            def _():
-                ids_copy(peer).start()
-
-        return c
+    heard(3)
+    for step in range(depth // 2):
+        tell(4 + 2 * step, up)
+        tell(5 + 2 * step, down)
+        if step == 0:
+            slot = (owner * cap + rank).astype(F32)
+            slots[...] = jnp.transpose(jnp.broadcast_to(slot, (128, rows)))
+        heard(4 + 2 * step)
+        heard(5 + 2 * step)
+    if depth < 2:
+        slot = (owner * cap + rank).astype(F32)
+        slots[...] = jnp.transpose(jnp.broadcast_to(slot, (128, rows)))
 
     lax.fori_loop(0, planes, send_ids, 0)
-
-    quarter = wide // 4
-
-    def a_part(c, k):
-        return pl.ds(pl.multiple_of(c * (2 * quarter) + k * quarter, quarter), quarter)
-
-    def a_half(c):
-        return pl.ds(pl.multiple_of(c * (2 * quarter), 2 * quarter), 2 * quarter)
-
-    lot = hidden // 8
-    lot2 = lot // 2
-
-    def b_lot(i):
-        return pl.ds(pl.multiple_of(i * lot, lot), lot)
-
-    def b_half(i, k):
-        return pl.ds(pl.multiple_of(i * lot + k * lot2, lot2), lot2)
-
-    in_r = [remote(win_hbm.at[a_part(core, k)], win.at[1, a_part(core, k)], dsend.at[k], drecv.at[k], RIGHT) for k in (0, 1)]
-    in_l = [remote(win_hbm.at[a_part(core, k)], win.at[2, a_part(core, k)], dsend.at[2 + k], drecv.at[2 + k], LEFT) for k in (0, 1)]
-    eighth = quarter // 2
-
-    def a_sub(c, k, j):
-        return pl.ds(pl.multiple_of(c * (2 * quarter) + k * quarter + j * eighth, eighth), eighth)
-
-    def a_on(k, j):
-        at = a_sub(core, k, j)
-        return remote(win.at[1 + k, at], win.at[3, at], dsend.at[4 + 2 * j + k], drecv.at[4 + 2 * j + k], (RIGHT, LEFT)[k])
-
-    def a_twin(c, k, j):
-        at = a_sub(c, k, j)
-        return remote(win.at[3, at], win.at[3, at], dsend.at[8 + 2 * j + k], drecv.at[8 + 2 * j + k], TWIN)
-
-    def a_twins(c):
-        both = win.at[pl.ds(1, 2), a_half(c)]
-        return remote(both, both, dsend.at[12], drecv.at[12], TWIN)
-
-    on = [[a_on(k, j) for k in (0, 1)] for j in (0, 1)]
-    twin_3 = [[a_twin(core, k, j) for k in (0, 1)] for j in (0, 1)]
-    twin_12 = a_twins(core)
-    lot_r = remote(wout_hbm.at[b_lot(p)], wout.at[1, b_lot(p)], ssend.at[0], srecv.at[0], RIGHT)
-    lot_l = remote(wout_hbm.at[b_lot(p)], wout.at[2, b_lot(p)], ssend.at[1], srecv.at[1], LEFT)
-    lot_on_r = remote(wout.at[1, b_half(p, 0)], wout.at[3, b_half(p, 0)], ssend.at[2], srecv.at[2], RIGHT)
-    lot_on_l = remote(wout.at[2, b_half(p, 1)], wout.at[3, b_half(p, 1)], ssend.at[3], srecv.at[3], LEFT)
-    slots_of = (pl.ds(1, 2), pl.ds(3, 1))
-
-    def share(m, at, i, where):
-        both = wout.at[slots_of[m], at]
-        return remote(both, both, ssend.at[4 + 8 * m + i], srecv.at[4 + 8 * m + i], where)
-
-    x_r = [share(m, b_lot(p), 0, XR) for m in (0, 1)]
-    x_l = [share(m, b_lot(p), 1, XL) for m in (0, 1)]
-    x_on_r = [share(m, b_half(p_l, 0), 2, XR) for m in (0, 1)]
-    x_on_l = [share(m, b_half(p_r, 1), 3, XL) for m in (0, 1)]
-    twins = [[share(m, b_lot(q), 4 + i, TWIN) for i, q in enumerate((p, p_l, p_r, p_x))] for m in (0, 1)]
-
-    def x_start(m):
-        x_r[m].start()
-        x_l[m].start()
-        twins[m][0].start()
-
-    def x_forward(m):
-        x_r[m].wait_recv()
-        x_l[m].wait_recv()
-        x_on_r[m].start()
-        x_on_l[m].start()
-        twins[m][1].start()
-        twins[m][2].start()
-
-    def x_finish(m):
-        x_on_r[m].wait_recv()
-        x_on_l[m].wait_recv()
-        twins[m][3].start()
-
-    lot_r.start()
-    lot_l.start()
-    in_r[0].start()
-    in_l[1].start()
-    q_back = remote(q_ref.at[pl.ds(0, GROUP)], qnext, hs.at[0], hr.at[0], {"seq": back})
     q_back.start()
     req[me] = want[me]
 
-    slot = (owner * cap + rank).astype(F32)
-    slots[...] = jnp.transpose(jnp.broadcast_to(slot, (128, rows)))
 
     def answer(i, c):
         to = lax.rem(mine + step_of(i), planes)
@@ -223,7 +237,7 @@
             def _():
                 ids_arrival(peer).wait_recv()
 
-        @pl.when(i == 2)
+        @pl.when(i == 0)
         def _():
             lot_r.wait_recv()
             lot_on_r.start()
@@ -265,7 +279,7 @@
     acc[...] = jnp.zeros_like(acc)
 
     def gather(i, c):
-        @pl.when(i == 1)
+        @pl.when(i == 0)
         def _():
             in_r[0].wait_recv()
             on[0][0].start()
@@ -274,17 +288,17 @@
             on[0][1].start()
             on[1][1].start()
 
-        @pl.when(i == 2)
+        @pl.when(i == 1)
         def _():
             lot_on_r.wait_recv()
             lot_on_l.wait_recv()
             x_start(1)
 
-        @pl.when(i == 5)
+        @pl.when(i == 3)
         def _():
             x_forward(0)
 
-        @pl.when(i == 6)
+        @pl.when(i == 5)
         def _():
             in_r[1].wait_recv()
             in_l[0].wait_recv()
@@ -492,7 +506,7 @@
             vm((GROUP, width)), vm((GROUP, width)),
             dma((4,)), dma((n,)), dma((n,)), dma((n,)), dma((n,)),
             dma((13,)), dma((13,)), dma((20,)), dma((20,)), dma((6,)), dma((6,)),
-            dma((groups, 4)), dma((groups, 4)), dma((2,)), dma((2,)),
+            dma((groups, 4)), dma((groups, 4)), dma((2,)), dma((2,)), pltpu.SemaphoreType.REGULAR((12,)),
         ],
         compiler_params=pltpu.CompilerParams(
             collective_id=0, has_side_effects=True, vmem_limit_bytes=58 * 1024 * 1024

time: 102 us -> 100 us (0.980)
  Pallas kernels: 99.3 us -> 96.9 us
    pallas_call x1, Pallas kernels: 99.3 us -> 96.9 us  [per_device(): pl.pallas_call(functools.partial(layer_kernel, n, groups, plane, cap), ou...]
where the time goes in v4:
time: 100 us; the launch traced here: 98.9 us
  Pallas kernels  96.9 us (97%)
  local copies, waits for them, and re-layouts  1.97 us (2%)
    pallas_call x1, Pallas kernels, per_device(): pl.pallas_call(functools.partial(layer_kernel, n, groups, plane, cap), ou...  96.9 us

profile of v4, /device:TPU:32, one launch (start us, length us, event | category | flops | bytes accessed | tf_op | source)
XLA Modules:
  0.0 98.9 jit_solution(8732037217474966287)
XLA Ops:
  0.0 96.9 %shard_map.73 = bf16[5,64,1024]{2,1,0:T(8,128)(2,1)} custom-call(s32[1,1024]{1,0:T(1,128)} %bitcast.3, bf16[2048,256]{1,0:T(8,128)(2,1)} %vocab_ref.1, bf16[256,1024]{1,0:T(8,128)(2,1)} %q_ref.1, bf16[1024,1024]{1,0:T(8,128)(2,1)} %win_hbm.1, bf16[1024,1024]{1,0:T(8,128)(2,1)} %wout_hbm.1, bf16[1024,1024]{1,0:T(8,128)(2,1)} %wk_hbm.1, bf16[1024,1024]{1,0:T(8,128)(2,1)} %wv_hbm.1), custom_call_target="tpu_custom_call" | custom-call | tf_op jit(solution)/shard_map/pallas_call | solution.py:494
  97.0 2.0 %slice.4 = bf16[256,1024]{1,0:T(8,128)(2,1)} slice(bf16[320,1024]{1,0:T(8,128)(2,1)} %bitcast.2), slice={[1:257], [0:1024]} | slice | bytes 1048576 | tf_op jit(solution)/shard_map/slice | solution.py:515
